TPU v7x, 32 devices: a whole 2x2x4 slice. The times are simulated.
32 devices in a mesh: req: 8 (over z, y), tp: 4 (over x, core).
Axes of the slice: x: 2, y: 2, z: 4, core: 2. Of those that a mesh axis runs over, the one named last changes fastest.
Arguments:
- tokens: bfloat16 [4096, 2048], P('req')
- token_request_number: int32 [8, 512], P('req'), may hold values from 0 to 7, never falling along the last dimension, each value on 1 to 256 neighbouring positions
- request_adapter_position: int32 [8, 8], P('req'), may hold values from 0 to 15
- adapters_in_use: int32 [16], replicated, may hold values from 0 to 15, as said below
- adapter_storage_slot: int32 [16], replicated, may hold values from 0 to 15, each once
- input_norm_gain: bfloat16 [2048], replicated, may hold values from 0.5 to 1.5
- query_weight: bfloat16 [2048, 2048], P('req', 'tp')
- key_weight: bfloat16 [2048, 2048], P('req', 'tp')
- value_weight: bfloat16 [2048, 2048], P('req', 'tp'), may hold values from -0.125 to 0.125
- output_weight: bfloat16 [2048, 2048], P('tp', 'req'), may hold values from -0.125 to 0.125
- adapter_down_weight: bfloat16 [16, 2, 16, 2048], P('req'), may hold values from -0.125 to 0.125
- adapter_up_weight: bfloat16 [16, 2, 16, 2048], P('req', None, None, 'tp'), may hold values from -0.75 to 0.75
Outputs:
- layer_out: bfloat16 [4096, 2048], P('req', 'tp')
Inputs may be any that keep to these rules, and one draw needn't show every extreme that they name: `adapters_in_use`: 16 different adapter numbers; 0 and 15 are always among them. `token_request_number`: the 512 tokens of each index of req form exactly 8 requests in order, each of 1 to 256 tokens, and one of exactly 256.
All inputs are finite; a program needn't handle non-finite values.
Results may differ from a plain program's by a relative error of at most 0.01.
Values may be sent and summed in bfloat16 or wider, within the bound.
A program may use at most 64 MiB of HBM per device.

v0:
```python
import jax
import jax.numpy as jnp
from jax import lax
from jax.sharding import PartitionSpec as P

HEAD_WIDTH = 64
norm_eps = 1e-05
rope_base = 130000.0
adapter_scale = 2.0


def fetch_adapters(down_part, up_part, active_slots, request_adapters, req_total):
    slot_total = down_part.shape[0]
    stored = jnp.concatenate([down_part, up_part], axis=1)
    split = down_part.shape[1]
    if slot_total * req_total <= 2 * active_slots.shape[0]:
        fetched = lax.all_gather(stored, "req", axis=0, tiled=True)
        places = active_slots[request_adapters]
    else:
        own = active_slots // slot_total == lax.axis_index("req")
        rows = jnp.where(
            own[:, None],
            jnp.take(stored, active_slots % slot_total, axis=0),
            jnp.zeros((), stored.dtype),
        )
        fetched = lax.psum(rows, "req")
        places = request_adapters
    return (fetched[:, :split], fetched[:, split:], places)


def positions_of(segment):
    ordinal = jnp.arange(segment.shape[0], dtype=jnp.int32)
    starts = jnp.concatenate([jnp.ones((1,), jnp.bool_), segment[1:] != segment[:-1]])
    segment_start = lax.cummax(jnp.where(starts, ordinal, jnp.zeros_like(ordinal)), axis=0)
    return ordinal - segment_start


def apply_rotation(values, token_positions):
    half_dim = HEAD_WIDTH // 2
    frequency = rope_base ** (-(jnp.arange(half_dim, dtype=jnp.float32) * 2.0 / HEAD_WIDTH))
    angles = token_positions.astype(jnp.float32)[:, None] * frequency[None, :]
    cosine = jnp.cos(angles)[:, None, :]
    sine_part = jnp.sin(angles)[:, None, :]
    first_half = values[..., :half_dim]
    second_half = values[..., half_dim:]
    return jnp.concatenate(
        [
            first_half * cosine - second_half * sine_part,
            second_half * cosine + first_half * sine_part,
        ],
        axis=-1,
    )


def attend(query_per_head, key_heads, value_per_head, segment):
    scores = (
        jnp.einsum("qhd,khd->hqk", query_per_head, key_heads, preferred_element_type=jnp.float32)
        * 0.125
    )
    ordinal = jnp.arange(segment.shape[0], dtype=jnp.int32)
    allowed = (segment[:, None] == segment[None, :]) & (ordinal[None, :] <= ordinal[:, None])
    scores = jnp.where(allowed[None], scores, jnp.float32(-1e30))
    row_peak = jnp.max(scores, axis=-1, keepdims=True)
    exponent = jnp.where(allowed[None], jnp.exp(scores - row_peak), jnp.float32(0.0))
    weights = (exponent / jnp.sum(exponent, axis=-1, keepdims=True)).astype(jnp.bfloat16)
    return jnp.einsum(
        "hqk,khd->qhd", weights, value_per_head, preferred_element_type=jnp.float32
    ).astype(jnp.bfloat16)


def local(
    tokens,
    token_request_number,
    request_adapter_position,
    adapters_in_use,
    adapter_storage_slot,
    input_norm_gain,
    query_weight,
    key_weight,
    value_weight,
    output_weight,
    adapter_down_weight,
    adapter_up_weight,
):
    row_total, model_width = tokens.shape
    local_width = query_weight.shape[1]
    reduced_rows = adapter_down_weight.shape[2]
    active_count = adapters_in_use.shape[0]
    slot_total = adapter_down_weight.shape[0]
    segment = token_request_number[0]
    request_adapters = request_adapter_position[0]
    tp_total = lax.axis_size("tp")
    req_total = lax.axis_size("req")
    part_rows = reduced_rows // tp_total
    down_part = lax.dynamic_slice_in_dim(
        adapter_down_weight, lax.axis_index("tp") * part_rows, part_rows, 2
    ).reshape(slot_total, 2 * part_rows * model_width)
    up_part = adapter_up_weight.reshape(slot_total, 2 * reduced_rows * local_width)
    down_all, up_all, request_places = fetch_adapters(
        down_part,
        up_part,
        jnp.take(adapter_storage_slot, adapters_in_use, axis=0),
        request_adapters,
        req_total,
    )
    place_total = down_all.shape[0]
    floats = tokens.astype(jnp.float32)
    normed = (
        floats
        * lax.rsqrt(jnp.mean(floats * floats, axis=-1, keepdims=True) + norm_eps)
        * input_norm_gain.astype(jnp.float32)
    ).astype(jnp.bfloat16)
    query_plain = jnp.dot(
        normed,
        lax.all_gather(query_weight, "req", axis=0, tiled=True),
        preferred_element_type=jnp.float32,
    )
    key_base = jnp.dot(
        normed,
        lax.all_gather(key_weight, "req", axis=0, tiled=True),
        preferred_element_type=jnp.float32,
    )
    value_plain = jnp.dot(
        normed,
        lax.all_gather(value_weight, "req", axis=0, tiled=True),
        preferred_element_type=jnp.float32,
    )
    request_total = request_adapters.shape[0]
    member = segment[:, None] == jnp.arange(request_total, dtype=jnp.int32)[None, :]
    token_place = jnp.sum(
        jnp.where(member, request_places[None, :], jnp.zeros_like(request_places)[None, :]), axis=1
    )
    share = 2 * part_rows
    shrunk_all = lax.dot_general(
        normed,
        down_all.reshape(place_total * share, model_width),
        (((1,), (1,)), ((), ())),
        preferred_element_type=jnp.float32,
    ).astype(jnp.bfloat16)
    column = jnp.arange(place_total * share, dtype=jnp.int32)
    kept = jnp.where(
        token_place[:, None] == (column // share)[None, :], shrunk_all, jnp.zeros((), jnp.bfloat16)
    )
    fold = (column % share)[:, None] == jnp.arange(share, dtype=jnp.int32)[None, :]
    shrunk_part = jnp.dot(
        kept, fold.astype(jnp.bfloat16), preferred_element_type=jnp.float32
    ).astype(jnp.bfloat16)
    shrunk = lax.all_gather(shrunk_part, "tp", axis=1, tiled=True)
    source = jnp.arange(tp_total * share, dtype=jnp.int32)
    source_kind = source % share // part_rows
    source_rank = source // share * part_rows + source % part_rows
    target = jnp.arange(place_total * reduced_rows, dtype=jnp.int32)
    mine = token_place[:, None] == (target // reduced_rows)[None, :]
    up_all = up_all.reshape(place_total, 2, reduced_rows, local_width)

    def change_of(kind):
        spread_map = (source_kind == kind)[:, None] & (
            source_rank[:, None] == (target % reduced_rows)[None, :]
        )
        spread = jnp.dot(
            shrunk, spread_map.astype(jnp.bfloat16), preferred_element_type=jnp.float32
        ).astype(jnp.bfloat16)
        spread = jnp.where(mine, spread, jnp.zeros((), jnp.bfloat16))
        return jnp.dot(
            spread,
            up_all[:, kind].reshape(place_total * reduced_rows, local_width),
            preferred_element_type=jnp.float32,
        )

    query_change = change_of(0)
    value_change = change_of(1)
    head_total = local_width // HEAD_WIDTH
    token_positions = positions_of(segment)
    query_per_head = apply_rotation(
        (query_plain + adapter_scale * query_change).reshape(row_total, head_total, HEAD_WIDTH),
        token_positions,
    ).astype(jnp.bfloat16)
    key_heads = apply_rotation(
        key_base.reshape(row_total, head_total, HEAD_WIDTH), token_positions
    ).astype(jnp.bfloat16)
    value_per_head = (
        (value_plain + adapter_scale * value_change)
        .astype(jnp.bfloat16)
        .reshape(row_total, head_total, HEAD_WIDTH)
    )
    attended = attend(query_per_head, key_heads, value_per_head, segment).reshape(
        row_total, local_width
    )
    partial_out = jnp.dot(
        attended,
        lax.all_gather(output_weight, "req", axis=1, tiled=True),
        preferred_element_type=jnp.float32,
    )
    summed = lax.psum_scatter(
        partial_out.astype(jnp.bfloat16), "tp", scatter_dimension=1, tiled=True
    ).astype(jnp.float32)
    share_width = summed.shape[1]
    residual_part = lax.dynamic_slice_in_dim(
        tokens, lax.axis_index("tp") * share_width, share_width, 1
    )
    return (summed + residual_part.astype(jnp.float32)).astype(jnp.bfloat16)


def solution(mesh):
    in_specs = (
        P("req", None),
        P("req", None),
        P("req", None),
        P(),
        P(),
        P(),
        P("req", "tp"),
        P("req", "tp"),
        P("req", "tp"),
        P("tp", "req"),
        P("req", None, None, None),
        P("req", None, None, "tp"),
    )
    out_specs = P("req", "tp")
    return jax.shard_map(local, mesh=mesh, in_specs=in_specs, out_specs=out_specs, check_vma=False)
```

profile of v0, /device:TPU:0, one launch (start us, length us, event | category | flops | bytes accessed | tf_op | source)
XLA Modules:
  0.0 296.7 jit_solution(14154784594400048160)
XLA Ops:
  6.5 0.0 all-gather.15.cloned.1.call-start
  6.6 1.0 copy.18
  7.7 0.1 reshape.292
  7.7 0.8 maximum_bitcast_fusion
  8.5 0.0 all-gather.7.cloned.1.call-start
  8.6 0.7 all-gather.7.cloned.1.call-update
  9.3 0.0 all-gather.9.cloned.1.call-start
  9.3 0.7 all-gather.9.cloned.1.call-update
  10.1 0.5 all-gather.11.cloned.1.call-update
  10.6 0.5 all-gather.13.cloned.1.call-update
  11.2 0.0 reduce-scatter.2.cloned.1.call-start
  11.3 0.7 convert_element_type.59
  12.0 2.1 fusion.2
  14.1 0.7 compare_select_fusion.1
  14.8 0.7 gather_fusion
  15.5 0.1 compare_reduce_fusion
  15.6 0.9 fusion.18
  16.5 0.6 gather_fusion.1
  17.1 0.1 select_reduce_fusion
  17.2 0.1 add_select_fusion
  17.3 0.3 reduce-window.9
  17.6 0.1 slice.46
  17.7 0.1 slice_reduce_fusion
  17.8 0.1 fusion.47
  17.9 0.9 multiply_cosine_fusion
  18.9 33.5 %all-gather.15.cloned.1.call-done = bf16[8,2,32768]{2,1,0:T(2,128)(2,1)} async-done(((bf16[1,2,32768]{2,1,0:T(2,128)(2,1)}), bf16[8,2,32768]{2,1,0:T(2,128)(2,1)}) %all-gather.15.cloned.1.call-update) | async-done | bytes 1048592 | tf_op jit(solution)/shard_map/all_gather | solution.py:17
  52.4 1.5 reshape.319
  53.9 0.9 fusion.70
  54.7 0.2 copy.19
  54.9 0.9 fusion.71
  55.8 1.3 reshape.294
  57.0 0.9 fusion.17
  58.0 5.4 %all_gather.20 = bf16[512,32]{0,1:T(8,128)(2,1)S(1)} all-gather(bf16[512,8]{0,1:T(8,128)(2,1)S(1)} %fusion.17), channel_id=1, replica_groups=mesh['req'=8,'tp'=4] {'tp'}, dimensions={1}, use_global_device_ids=true | all-gather | bytes 40960 | tf_op jit(solution)/shard_map/all_gather | solution.py:148
  63.4 39.2 %all-gather.7.cloned.1.call-done = bf16[2048,512]{1,0:T(8,128)(2,1)} async-done(((bf16[256,512]{1,0:T(8,128)(2,1)}), bf16[2048,512]{1,0:T(8,128)(2,1)}) %all-gather.7.cloned.1.call-update) | async-done | bytes 2097168 | tf_op jit(solution)/shard_map/all_gather | solution.py:125
  102.6 3.0 %fusion.68 = f32[512,512]{0,1:T(8,128)S(1)} fusion(bf16[2048,512]{1,0:T(8,128)(2,1)} %all-gather.7.cloned.1.call-done, bf16[512,2048]{1,0:T(8,128)(2,1)S(1)} %copy-done.2, f32[2048]{0:T(1024)S(1)} %convert_element_type.59, f32[512]{0:T(512)S(1)} %add_rsqrt_fusion), kind=kOutput, calls=%fused_computation.120 | convolution fusion | flops 1077936128 | bytes 5253120 | tf_op jit(solution)/shard_map/dot_general | solution.py:123
  105.6 2.3 fusion.12
  107.9 44.7 %all-gather.9.cloned.1.call-done = bf16[2048,512]{1,0:T(8,128)(2,1)} async-done(((bf16[256,512]{1,0:T(8,128)(2,1)}), bf16[2048,512]{1,0:T(8,128)(2,1)}) %all-gather.9.cloned.1.call-update) | async-done | bytes 2097168 | tf_op jit(solution)/shard_map/all_gather | solution.py:115
  152.5 3.9 %fusion.64 = f32[512,512]{0,1:T(8,128)} fusion(bf16[2048,512]{1,0:T(8,128)(2,1)} %all-gather.9.cloned.1.call-done, bf16[512,2048]{1,0:T(8,128)(2,1)S(1)} %copy-done.2, f32[2048]{0:T(1024)S(1)} %convert_element_type.59, f32[512]{0:T(512)S(1)} %add_rsqrt_fusion), kind=kOutput, calls=%fused_computation.119 | convolution fusion | flops 1077936128 | bytes 5253120 | tf_op jit(solution)/shard_map/dot_general | solution.py:113
  156.5 1.9 fusion.9
  158.4 44.0 %all-gather.11.cloned.1.call-done = bf16[2048,512]{1,0:T(8,128)(2,1)} async-done(((bf16[256,512]{1,0:T(8,128)(2,1)}), bf16[2048,512]{1,0:T(8,128)(2,1)}) %all-gather.11.cloned.1.call-update) | async-done | bytes 2097168 | tf_op jit(solution)/shard_map/all_gather | solution.py:120
  202.3 3.0 %fusion.62 = f32[512,512]{0,1:T(8,128)S(1)} fusion(bf16[2048,512]{1,0:T(8,128)(2,1)} %all-gather.11.cloned.1.call-done, bf16[512,2048]{1,0:T(8,128)(2,1)S(1)} %copy-done.2, f32[2048]{0:T(1024)S(1)} %convert_element_type.59, f32[512]{0:T(512)S(1)} %add_rsqrt_fusion), kind=kOutput, calls=%fused_computation.118 | convolution fusion | flops 1077936128 | bytes 5253120 | tf_op jit(solution)/shard_map/dot_general | solution.py:118
  205.4 1.3 subtract_convert_fusion.1
  206.7 8.2 %fusion.72 = (f32[8,512]{1,0:T(8,128)S(1)}, f32[8,512,512]{1,2,0:T(8,128)}) fusion(pred[512,512]{0,1:T(8,128)(4,1)} %fusion.18, bf16[512,8,32]{0,2,1:T(8,128)(2,1)} %get-tuple-element.13, bf16[512,8,32]{0,2,1:T(8,128)(2,1)} %get-tuple-element.14, bf16[512,8,32]{0,2,1:T(8,128)(2,1)} %get-tuple-element.6, bf16[512,8,32]{0,2,1:T(8,128)(2,1)} %get-tuple-element.5), kind=kOutput, calls=%fused_computation.123 | convolution fusion | flops 281018880 | bytes 9715712 | tf_op jit(solution)/shard_map/sub | solution.py:64
  214.9 4.3 %fusion.11 = bf16[8,64,512]{2,1,0:T(8,128)(2,1)S(1)} fusion(bf16[512,8,64]{0,2,1:T(8,128)(2,1)S(1)} %bitcast.46, f32[8,512,512]{1,2,0:T(8,128)} %get-tuple-element.18, f32[8,512]{1,0:T(8,128)S(1)} %get-tuple-element.17), kind=kOutput, calls=%fused_computation.21 | convolution fusion | flops 272891904 | bytes 9453568 | tf_op jit(solution)/shard_map/hqk,khd->qhd/dot_general | solution.py:66
  219.2 34.7 %all-gather.13.cloned.1.call-done = bf16[512,2048]{1,0:T(8,128)(2,1)} async-done(((bf16[512,256]{1,0:T(8,128)(2,1)}), bf16[512,2048]{1,0:T(8,128)(2,1)}) %all-gather.13.cloned.1.call-update) | async-done | bytes 2097168 | tf_op jit(solution)/shard_map/all_gather | solution.py:191
  253.8 4.2 %convolution_convert_fusion = bf16[512,2048]{1,0:T(8,128)(2,1)} fusion(bf16[512,512]{0,1:T(8,128)(2,1)S(1)} %bitcast.51, bf16[512,2048]{1,0:T(8,128)(2,1)} %all-gather.13.cloned.1.call-done), kind=kOutput, calls=%fused_computation.16 | convolution fusion | flops 1074790400 | bytes 4718592 | tf_op jit(solution)/shard_map/dot_general | solution.py:189
  258.1 29.8 %reduce-scatter.2.cloned.1.call-done = bf16[512,512]{1,0:T(8,128)(2,1)} async-done(((bf16[512,2048]{1,0:T(8,128)(2,1)}), bf16[512,512]{1,0:T(8,128)(2,1)}) %reduce-scatter.2.cloned.1.call-update) | async-done | bytes 524304 | tf_op jit(solution)/shard_map/reduce_scatter | solution.py:194
  287.8 2.0 add_convert_fusion
  (33 shorter events, 0.3 us)
Async XLA Ops:
  6.5 1.1 copy-start
  6.5 8.9 %copy-start.6 = (s32[16]{0:T(128)S(1)}, s32[16]{0:T(128)}, u32[]{:S(2)}) copy-start(s32[16]{0:T(128)} %param.15) | copy-start | bytes 196
  6.5 8.2 %copy-start.1 = (s32[16]{0:T(128)S(1)}, s32[16]{0:T(128)}, u32[]{:S(2)}) copy-start(s32[16]{0:T(128)} %param.16) | copy-start | bytes 196
  6.5 8.9 %copy-start.7 = (s32[1,8]{1,0:T(1,128)S(1)}, s32[1,8]{1,0:T(1,128)}, u32[]{:S(2)}) copy-start(s32[1,8]{1,0:T(1,128)} %param.14) | copy-start | bytes 100
  6.5 8.9 %copy-start.5 = (s32[1,512]{1,0:T(1,128)S(1)}, s32[1,512]{1,0:T(1,128)}, u32[]{:S(2)}) copy-start(s32[1,512]{1,0:T(1,128)} %param.13) | copy-start | bytes 6148
  6.5 45.8 %all-gather.15.cloned.1.call-start = ((), (), s32[]{:S(2)}) async-start(), calls=%async_computation.6 | async-start | bytes 1179648 | tf_op jit(solution)/shard_map/all_gather | solution.py:17
  8.5 94.1 %all-gather.7.cloned.1.call-start = ((), (), s32[]{:S(2)}) async-start(), calls=%async_computation.1 | async-start | bytes 2359296 | tf_op jit(solution)/shard_map/all_gather | solution.py:125
  9.3 143.3 %all-gather.9.cloned.1.call-start = ((), (), s32[]{:S(2)}) async-start(), calls=%async_computation.2 | async-start | bytes 2359296 | tf_op jit(solution)/shard_map/all_gather | solution.py:115
  10.0 192.3 %all-gather.11.cloned.1.call-start = ((), (), s32[]{:S(2)}) async-start(), calls=%async_computation.3 | async-start | bytes 2359296 | tf_op jit(solution)/shard_map/all_gather | solution.py:120
  10.6 243.2 %all-gather.13.cloned.1.call-start = ((), (), s32[]{:S(2)}) async-start(), calls=%async_computation.4 | async-start | bytes 2359296 | tf_op jit(solution)/shard_map/all_gather | solution.py:191
  11.2 276.6 %reduce-scatter.2.cloned.1.call-start = ((), (), s32[]{:S(2)}) async-start(), calls=%async_computation.5 | async-start | bytes 2621440 | tf_op jit(solution)/shard_map/reduce_scatter | solution.py:194
  15.4 41.6 %copy-start.2 = (bf16[512,2048]{1,0:T(8,128)(2,1)S(1)}, bf16[512,2048]{1,0:T(8,128)(2,1)}, u32[]{:S(2)}) copy-start(bf16[512,2048]{1,0:T(8,128)(2,1)} %param.12) | copy-start | bytes 6291460
  202.3 3.0 %copy-start.4 = (f32[512,32]{0,1:T(8,128)S(1)}, f32[512,32]{0,1:T(8,128)}, u32[]{:S(2)}) copy-start(f32[512,32]{0,1:T(8,128)} %get-tuple-element.16) | copy-start | bytes 196612
  206.7 8.2 %copy-start.3 = (bf16[512,512]{0,1:T(8,128)(2,1)S(1)}, bf16[512,512]{0,1:T(8,128)(2,1)}, u32[]{:S(2)}) copy-start(bf16[512,512]{0,1:T(8,128)(2,1)} %fusion.12) | copy-start | bytes 1572868
Sparse Core Ops, SparseCore 0:
  9.5 42.8 all-gather.14
  54.5 48.0 all-gather.6
  104.7 47.7 all-gather.8
  154.5 47.7 all-gather.10
  204.2 49.5 all-gather.12
  258.2 29.5 reduce-scatter.1
where the time goes:
time: 297 us
  waiting for transfers between devices  228 us (77%)
  matrix products  31.7 us (11%)
  between operations  13.7 us (5%)
  other arithmetic  10.1 us (3%)
  local copies, waits for them, and re-layouts  7.27 us (2%)
  blocking collectives  5.39 us (2%)
    all_gather x1, waiting for transfers between devices, local(): lax.all_gather(query_weight, 'req', axis=0, tiled=True)  44.7 us
    all_gather x1, waiting for transfers between devices, local(): lax.all_gather(key_weight, 'req', axis=0, tiled=True)  44 us
    all_gather x1, waiting for transfers between devices, local(): lax.all_gather(value_weight, 'req', axis=0, tiled=True)  39.2 us
    all_gather x1, waiting for transfers between devices, local(): lax.all_gather(output_weight, 'req', axis=1, tiled=True)  34.7 us
    all_gather x1, waiting for transfers between devices, fetch_adapters(): fetched = lax.all_gather(stored, 'req', axis=0, tiled=True)  33.5 us
    reduce_scatter x1, waiting for transfers between devices, local(): lax.psum_scatter(partial_out.astype(jnp.bfloat16), 'tp', scatter_dimensio...  29.8 us
    sub x1, matrix products, attend(): scores - row_peak  8.2 us
  transfers between devices with their start and end apart: 6, of which 6 were waited for; matrix products, arithmetic and copies ran while one was open for 14% of the time, Pallas kernels for 0%

commit v1 on v0

--- a/solution.py
+++ b/solution.py
@@ -7,6 +7,17 @@
 norm_eps = 1e-05
 rope_base = 130000.0
 adapter_scale = 2.0
+
+
+def around_the_ring(block, axis, d):
+    size = lax.axis_size(axis)
+    right = [(i, (i + 1) % size) for i in range(size)]
+    blocks = [block]
+    for stride in range(1, size):
+        blocks = [lax.ppermute(blocks[0], axis, right), *blocks]
+    full = jnp.concatenate(blocks, axis=d)
+    shift = (lax.axis_index(axis) + 1) * blocks[-1].shape[d]
+    return jnp.roll(full, shift, axis=d)
 
 
 def fetch_adapters(down_part, up_part, active_slots, request_adapters, req_total):
@@ -14,7 +25,7 @@
     stored = jnp.concatenate([down_part, up_part], axis=1)
     split = down_part.shape[1]
     if slot_total * req_total <= 2 * active_slots.shape[0]:
-        fetched = lax.all_gather(stored, "req", axis=0, tiled=True)
+        fetched = around_the_ring(stored, "req", 0)
         places = active_slots[request_adapters]
     else:
         own = active_slots // slot_total == lax.axis_index("req")

time: 297 us -> 266 us (0.90)
  waiting for transfers between devices: 228 us -> 195 us
  starting transfers between devices: 0.23 us -> 3.23 us
    ppermute x0 -> x7, waiting for transfers between devices: none -> 56 us  [around_the_ring(): blocks = [lax.ppermute(blocks[0], axis, right), *blocks]]
    all_gather x1, waiting for transfers between devices: 39.2 us -> 0.01 us  [local(): lax.all_gather(value_weight, 'req', axis=0, tiled=True)]
    all_gather x1 -> x0, waiting for transfers between devices: 33.5 us -> none  [fetch_adapters(): fetched = lax.all_gather(stored, 'req', axis=0, tiled=True)]
    all_gather x1, waiting for transfers between devices: 44.7 us -> 28.6 us  [local(): lax.all_gather(query_weight, 'req', axis=0, tiled=True)]
    concatenate x0 -> x2, local copies, waits for them, and re-layouts: none -> 3.43 us  [the longest x1 3.37 us: around_the_ring(): return jnp.roll(full, shift, axis=d)]
    ppermute x0 -> x7, starting transfers between devices: none -> 3.03 us  [around_the_ring(): blocks = [lax.ppermute(blocks[0], axis, right), *blocks]]
  transfers between devices with their start and end apart: 6 -> 12, of which waited for: 6 -> 11; matrix products, arithmetic and copies ran while one was open for 14% -> 15% of each run, Pallas kernels for 0% -> 0%
where the time goes in v1:
time: 266 us; the launch traced here: 265 us
  waiting for transfers between devices  195 us (73%)
  matrix products  31.7 us (12%)
  between operations  13.4 us (5%)
  local copies, waits for them, and re-layouts  8.23 us (3%)
  other arithmetic  8 us (3%)
  blocking collectives  5.64 us (2%)
  starting transfers between devices  3.23 us (1%)
    ppermute x7, waiting for transfers between devices, around_the_ring(): blocks = [lax.ppermute(blocks[0], axis, right), *blocks]  56 us
    all_gather x1, waiting for transfers between devices, local(): lax.all_gather(key_weight, 'req', axis=0, tiled=True)  44.1 us
    all_gather x1, waiting for transfers between devices, local(): lax.all_gather(output_weight, 'req', axis=1, tiled=True)  34.7 us
    reduce_scatter x1, waiting for transfers between devices, local(): lax.psum_scatter(partial_out.astype(jnp.bfloat16), 'tp', scatter_dimensio...  29.8 us
    all_gather x1, waiting for transfers between devices, local(): lax.all_gather(query_weight, 'req', axis=0, tiled=True)  28.6 us
    sub x1, matrix products, attend(): scores - row_peak  8.19 us
    all_gather x1, blocking collectives, local(): shrunk = lax.all_gather(shrunk_part, 'tp', axis=1, tiled=True)  5.64 us
  transfers between devices with their start and end apart: 12, of which 11 were waited for; matrix products, arithmetic and copies ran while one was open for 15% of the time, Pallas kernels for 0%

profile of v1, /device:TPU:0, one launch (start us, length us, event | category | flops | bytes accessed | tf_op | source)
XLA Modules:
  0.0 265.4 jit_solution(17502435717379172334)
XLA Ops:
  6.6 0.7 all-gather.5.cloned.1.call-update
  7.3 0.7 all-gather.7.cloned.1.call-update
  8.1 0.7 all-gather.9.cloned.1.call-update
  8.9 0.1 reshape.292
  9.0 0.9 copy.17
  9.9 0.1 constant_dynamic-update-slice_fusion
  10.0 3.0 %collective-permute-start = (bf16[2,32768]{1,0:T(2,128)(2,1)S(1)}, bf16[2,32768]{1,0:T(2,128)(2,1)S(1)}, u32[]{:S(2)}, u32[]{:S(2)}) collective-permute-start(bf16[2,32768]{1,0:T(2,128)(2,1)S(1)} %constant_dynamic-update-slice_fusion), channel_id=1, source_target_pairs={{0,4},{4,8},{8,12},{12,16},{16,20},{20,24},{24,28},{28,0},{1,5},{5... | collective-permute-start | bytes 393224 | tf_op jit(solution)/shard_map/ppermute | solution.py:17
  13.1 2.1 fusion.2
  15.2 0.1 compare_reduce_fusion
  15.3 0.9 fusion.18
  16.2 0.1 add_select_fusion
  16.3 0.3 reduce-window.9
  16.6 0.1 slice.46
  16.7 0.1 slice_reduce_fusion
  16.8 0.1 fusion.47
  16.9 0.7 gather_fusion
  17.6 1.9 collective-permute-done
  19.6 0.9 multiply_cosine_fusion
  20.5 9.5 %collective-permute-done.1 = bf16[2,32768]{1,0:T(2,128)(2,1)S(1)} collective-permute-done((bf16[2,32768]{1,0:T(2,128)(2,1)S(1)}, bf16[2,32768]{1,0:T(2,128)(2,1)S(1)}, u32[]{:S(2)}, u32[]{:S(2)}) %collective-permute-start.1) | collective-permute-done | bytes 131104 | tf_op jit(solution)/shard_map/ppermute | solution.py:17
  30.1 8.4 %collective-permute-done.2 = bf16[2,32768]{1,0:T(2,128)(2,1)S(1)} collective-permute-done((bf16[2,32768]{1,0:T(2,128)(2,1)S(1)}, bf16[2,32768]{1,0:T(2,128)(2,1)S(1)}, u32[]{:S(2)}, u32[]{:S(2)}) %collective-permute-start.2) | collective-permute-done | bytes 131104 | tf_op jit(solution)/shard_map/ppermute | solution.py:17
  38.5 7.8 %collective-permute-done.3 = bf16[2,32768]{1,0:T(2,128)(2,1)S(1)} collective-permute-done((bf16[2,32768]{1,0:T(2,128)(2,1)S(1)}, bf16[2,32768]{1,0:T(2,128)(2,1)S(1)}, u32[]{:S(2)}, u32[]{:S(2)}) %collective-permute-start.3) | collective-permute-done | bytes 131104 | tf_op jit(solution)/shard_map/ppermute | solution.py:17
  46.3 11.1 %collective-permute-done.4 = bf16[2,32768]{1,0:T(2,128)(2,1)S(1)} collective-permute-done((bf16[2,32768]{1,0:T(2,128)(2,1)S(1)}, bf16[2,32768]{1,0:T(2,128)(2,1)S(1)}, u32[]{:S(2)}, u32[]{:S(2)}) %collective-permute-start.4) | collective-permute-done | bytes 131104 | tf_op jit(solution)/shard_map/ppermute | solution.py:17
  57.4 10.4 %collective-permute-done.5 = bf16[2,32768]{1,0:T(2,128)(2,1)S(1)} collective-permute-done((bf16[2,32768]{1,0:T(2,128)(2,1)S(1)}, bf16[2,32768]{1,0:T(2,128)(2,1)S(1)}, u32[]{:S(2)}, u32[]{:S(2)}) %collective-permute-start.5) | collective-permute-done | bytes 131104 | tf_op jit(solution)/shard_map/ppermute | solution.py:17
  67.8 0.6 gather_fusion.1
  68.5 0.1 select_reduce_fusion
  68.6 6.9 %collective-permute-done.6 = bf16[2,32768]{1,0:T(2,128)(2,1)S(1)} collective-permute-done((bf16[2,32768]{1,0:T(2,128)(2,1)S(1)}, bf16[2,32768]{1,0:T(2,128)(2,1)S(1)}, u32[]{:S(2)}, u32[]{:S(2)}) %collective-permute-start.6) | collective-permute-done | bytes 131104 | tf_op jit(solution)/shard_map/ppermute | solution.py:17
  75.4 3.4 %concatenate.23 = bf16[32,32768]{1,0:T(8,128)(2,1)S(1)} concatenate(bf16[2,32768]{1,0:T(2,128)(2,1)S(1)} %collective-permute-done.6, bf16[2,32768]{1,0:T(2,128)(2,1)S(1)} %collective-permute-done.5, bf16[2,32768]{1,0:T(2,128)(2,1)S(1)} %collective-permute-done.4, bf16[2,32768]{1,0:T(2,128)(2,1)S(1)} %collective-permute-done.3, bf16[2,32768]{1,0:T(2,128)(2,1)S(1)} %collective-permute-done.2, ...), dimensions={0} | concatenate | bytes 4194304 | tf_op jit(solution)/shard_map/jit(_roll_dynamic)/concatenate | solution.py:20
  78.8 0.4 constant_dynamic-slice_fusion.1
  79.2 0.2 copy.18
  79.4 0.8 fusion.70
  80.2 0.2 reshape.294
  80.5 0.6 copy-done.2
  81.0 0.9 fusion.17
  82.0 5.6 %all_gather.16 = bf16[512,32]{0,1:T(8,128)(2,1)S(1)} all-gather(bf16[512,8]{0,1:T(8,128)(2,1)S(1)} %fusion.17), channel_id=1, replica_groups=mesh['req'=8,'tp'=4] {'tp'}, dimensions={1}, use_global_device_ids=true | all-gather | bytes 40960 | tf_op jit(solution)/shard_map/all_gather | solution.py:159
  87.6 3.0 %fusion.68 = f32[512,512]{0,1:T(8,128)S(1)} fusion(bf16[2048,512]{1,0:T(8,128)(2,1)} %all-gather.5.cloned.1.call-done, bf16[512,2048]{1,0:T(8,128)(2,1)S(1)} %copy-done.2, f32[2048]{0:T(1024)S(1)} %convert_element_type.59, f32[512]{0:T(512)S(1)} %add_rsqrt_fusion), kind=kOutput, calls=%fused_computation.122 | convolution fusion | flops 1077936128 | bytes 5253120 | tf_op jit(solution)/shard_map/dot_general | solution.py:134
  90.6 2.3 fusion.12
  92.9 28.6 %all-gather.7.cloned.1.call-done = bf16[2048,512]{1,0:T(8,128)(2,1)} async-done(((bf16[256,512]{1,0:T(8,128)(2,1)}), bf16[2048,512]{1,0:T(8,128)(2,1)}) %all-gather.7.cloned.1.call-update) | async-done | bytes 2097168 | tf_op jit(solution)/shard_map/all_gather | solution.py:126
  121.5 3.9 %fusion.64 = f32[512,512]{0,1:T(8,128)} fusion(bf16[2048,512]{1,0:T(8,128)(2,1)} %all-gather.7.cloned.1.call-done, bf16[512,2048]{1,0:T(8,128)(2,1)S(1)} %copy-done.2, f32[2048]{0:T(1024)S(1)} %convert_element_type.59, f32[512]{0:T(512)S(1)} %add_rsqrt_fusion), kind=kOutput, calls=%fused_computation.121 | convolution fusion | flops 1077936128 | bytes 5253120 | tf_op jit(solution)/shard_map/dot_general | solution.py:124
  125.4 1.9 fusion.9
  127.3 44.1 %all-gather.9.cloned.1.call-done = bf16[2048,512]{1,0:T(8,128)(2,1)} async-done(((bf16[256,512]{1,0:T(8,128)(2,1)}), bf16[2048,512]{1,0:T(8,128)(2,1)}) %all-gather.9.cloned.1.call-update) | async-done | bytes 2097168 | tf_op jit(solution)/shard_map/all_gather | solution.py:131
  171.4 3.0 %fusion.62 = f32[512,512]{0,1:T(8,128)S(1)} fusion(bf16[2048,512]{1,0:T(8,128)(2,1)} %all-gather.9.cloned.1.call-done, bf16[512,2048]{1,0:T(8,128)(2,1)S(1)} %copy-done.2, f32[2048]{0:T(1024)S(1)} %convert_element_type.59, f32[512]{0:T(512)S(1)} %add_rsqrt_fusion), kind=kOutput, calls=%fused_computation.120 | convolution fusion | flops 1077936128 | bytes 5253120 | tf_op jit(solution)/shard_map/dot_general | solution.py:129
  174.4 1.3 subtract_convert_fusion.1
  175.7 8.2 %fusion.71 = (f32[8,512]{1,0:T(8,128)S(1)}, f32[8,512,512]{1,2,0:T(8,128)}) fusion(pred[512,512]{0,1:T(8,128)(4,1)} %fusion.18, bf16[512,8,32]{0,2,1:T(8,128)(2,1)} %get-tuple-element.13, bf16[512,8,32]{0,2,1:T(8,128)(2,1)} %get-tuple-element.14, bf16[512,8,32]{0,2,1:T(8,128)(2,1)} %get-tuple-element.8, bf16[512,8,32]{0,2,1:T(8,128)(2,1)} %get-tuple-element.7), kind=kOutput, calls=%fused_computation.124 | convolution fusion | flops 281018880 | bytes 9715712 | tf_op jit(solution)/shard_map/sub | solution.py:75
  183.9 4.2 %fusion.11 = bf16[8,64,512]{2,1,0:T(8,128)(2,1)S(1)} fusion(bf16[512,8,64]{0,2,1:T(8,128)(2,1)S(1)} %bitcast.44, f32[8,512,512]{1,2,0:T(8,128)} %get-tuple-element.18, f32[8,512]{1,0:T(8,128)S(1)} %get-tuple-element.17), kind=kOutput, calls=%fused_computation.21 | convolution fusion | flops 272891904 | bytes 9453568 | tf_op jit(solution)/shard_map/hqk,khd->qhd/dot_general | solution.py:77
  188.2 34.7 %all-gather.11.cloned.1.call-done = bf16[512,2048]{1,0:T(8,128)(2,1)} async-done(((bf16[512,256]{1,0:T(8,128)(2,1)}), bf16[512,2048]{1,0:T(8,128)(2,1)}) %all-gather.11.cloned.1.call-update) | async-done | bytes 2097168 | tf_op jit(solution)/shard_map/all_gather | solution.py:202
  222.9 4.2 %convolution_convert_fusion = bf16[512,2048]{1,0:T(8,128)(2,1)} fusion(bf16[512,512]{0,1:T(8,128)(2,1)S(1)} %bitcast.49, bf16[512,2048]{1,0:T(8,128)(2,1)} %all-gather.11.cloned.1.call-done), kind=kOutput, calls=%fused_computation.16 | convolution fusion | flops 1074790400 | bytes 4718592 | tf_op jit(solution)/shard_map/dot_general | solution.py:200
  227.1 29.8 %reduce-scatter.2.cloned.1.call-done = bf16[512,512]{1,0:T(8,128)(2,1)} async-done(((bf16[512,2048]{1,0:T(8,128)(2,1)}), bf16[512,512]{1,0:T(8,128)(2,1)}) %reduce-scatter.2.cloned.1.call-update) | async-done | bytes 524304 | tf_op jit(solution)/shard_map/reduce_scatter | solution.py:205
  256.9 2.0 add_convert_fusion
  (46 shorter events, 0.5 us)
Async XLA Ops:
  6.5 2.3 copy-start
  6.5 8.6 %copy-start.7 = (s32[1,8]{1,0:T(1,128)S(1)}, s32[1,8]{1,0:T(1,128)}, u32[]{:S(2)}) copy-start(s32[1,8]{1,0:T(1,128)} %param.14) | copy-start | bytes 100
  6.5 8.7 %copy-start.8 = (s32[16]{0:T(128)S(1)}, s32[16]{0:T(128)}, u32[]{:S(2)}) copy-start(s32[16]{0:T(128)} %param.15) | copy-start | bytes 196
  6.5 8.7 %copy-start.5 = (s32[1,512]{1,0:T(1,128)S(1)}, s32[1,512]{1,0:T(1,128)}, u32[]{:S(2)}) copy-start(s32[1,512]{1,0:T(1,128)} %param.13) | copy-start | bytes 6148
  6.5 10.4 %copy-start.1 = (s32[16]{0:T(128)S(1)}, s32[16]{0:T(128)}, u32[]{:S(2)}) copy-start(s32[16]{0:T(128)} %param.16) | copy-start | bytes 196
  6.5 81.1 %all-gather.5.cloned.1.call-start = ((), (), s32[]{:S(2)}) async-start(), calls=%async_computation.1 | async-start | bytes 2359296 | tf_op jit(solution)/shard_map/all_gather | solution.py:136
  7.3 114.2 %all-gather.7.cloned.1.call-start = ((), (), s32[]{:S(2)}) async-start(), calls=%async_computation.2 | async-start | bytes 2359296 | tf_op jit(solution)/shard_map/all_gather | solution.py:126
  8.0 59.8 %copy-start.6 = (bf16[2048]{0:T(1024)(128)(2,1)S(1)}, bf16[2048]{0:T(1024)(128)(2,1)}, u32[]{:S(2)}) copy-start(bf16[2048]{0:T(1024)(128)(2,1)} %param.17) | copy-start | bytes 12292
  8.0 163.4 %all-gather.9.cloned.1.call-start = ((), (), s32[]{:S(2)}) async-start(), calls=%async_computation.3 | async-start | bytes 2359296 | tf_op jit(solution)/shard_map/all_gather | solution.py:131
  8.8 214.1 %all-gather.11.cloned.1.call-start = ((), (), s32[]{:S(2)}) async-start(), calls=%async_computation.4 | async-start | bytes 2359296 | tf_op jit(solution)/shard_map/all_gather | solution.py:202
  10.0 9.6 %collective-permute-start = (bf16[2,32768]{1,0:T(2,128)(2,1)S(1)}, bf16[2,32768]{1,0:T(2,128)(2,1)S(1)}, u32[]{:S(2)}, u32[]{:S(2)}) collective-permute-start(bf16[2,32768]{1,0:T(2,128)(2,1)S(1)} %constant_dynamic-update-slice_fusion), channel_id=1, source_target_pairs={{0,4},{4,8},{8,12},{12,16},{16,20},{20,24},{24,28},{28,0},{1,5},{5... | collective-permute-start | bytes 393224 | tf_op jit(solution)/shard_map/ppermute | solution.py:17
  13.0 243.8 %reduce-scatter.2.cloned.1.call-start = ((), (), s32[]{:S(2)}) async-start(), calls=%async_computation.5 | async-start | bytes 2621440 | tf_op jit(solution)/shard_map/reduce_scatter | solution.py:205
  19.6 10.5 %collective-permute-start.1 = (bf16[2,32768]{1,0:T(2,128)(2,1)S(1)}, bf16[2,32768]{1,0:T(2,128)(2,1)S(1)}, u32[]{:S(2)}, u32[]{:S(2)}) collective-permute-start(bf16[2,32768]{1,0:T(2,128)(2,1)S(1)} %collective-permute-done), channel_id=1, source_target_pairs={{0,4},{4,8},{8,12},{12,16},{16,20},{20,24},{24,28},{28,0},{1,5},{5... | collective-permute-start | bytes 393224 | tf_op jit(solution)/shard_map/ppermute | solution.py:17
  30.0 8.4 %collective-permute-start.2 = (bf16[2,32768]{1,0:T(2,128)(2,1)S(1)}, bf16[2,32768]{1,0:T(2,128)(2,1)S(1)}, u32[]{:S(2)}, u32[]{:S(2)}) collective-permute-start(bf16[2,32768]{1,0:T(2,128)(2,1)S(1)} %collective-permute-done.1), channel_id=1, source_target_pairs={{0,4},{4,8},{8,12},{12,16},{16,20},{20,24},{24,28},{28,0},{1,5},{5... | collective-permute-start | bytes 393224 | tf_op jit(solution)/shard_map/ppermute | solution.py:17
  38.4 7.8 %collective-permute-start.3 = (bf16[2,32768]{1,0:T(2,128)(2,1)S(1)}, bf16[2,32768]{1,0:T(2,128)(2,1)S(1)}, u32[]{:S(2)}, u32[]{:S(2)}) collective-permute-start(bf16[2,32768]{1,0:T(2,128)(2,1)S(1)} %collective-permute-done.2), channel_id=1, source_target_pairs={{0,4},{4,8},{8,12},{12,16},{16,20},{20,24},{24,28},{28,0},{1,5},{5... | collective-permute-start | bytes 393224 | tf_op jit(solution)/shard_map/ppermute | solution.py:17
  46.3 11.2 %collective-permute-start.4 = (bf16[2,32768]{1,0:T(2,128)(2,1)S(1)}, bf16[2,32768]{1,0:T(2,128)(2,1)S(1)}, u32[]{:S(2)}, u32[]{:S(2)}) collective-permute-start(bf16[2,32768]{1,0:T(2,128)(2,1)S(1)} %collective-permute-done.3), channel_id=1, source_target_pairs={{0,4},{4,8},{8,12},{12,16},{16,20},{20,24},{24,28},{28,0},{1,5},{5... | collective-permute-start | bytes 393224 | tf_op jit(solution)/shard_map/ppermute | solution.py:17
  57.4 10.4 %collective-permute-start.5 = (bf16[2,32768]{1,0:T(2,128)(2,1)S(1)}, bf16[2,32768]{1,0:T(2,128)(2,1)S(1)}, u32[]{:S(2)}, u32[]{:S(2)}) collective-permute-start(bf16[2,32768]{1,0:T(2,128)(2,1)S(1)} %collective-permute-done.4), channel_id=1, source_target_pairs={{0,4},{4,8},{8,12},{12,16},{16,20},{20,24},{24,28},{28,0},{1,5},{5... | collective-permute-start | bytes 393224 | tf_op jit(solution)/shard_map/ppermute | solution.py:17
  67.8 7.7 %collective-permute-start.6 = (bf16[2,32768]{1,0:T(2,128)(2,1)S(1)}, bf16[2,32768]{1,0:T(2,128)(2,1)S(1)}, u32[]{:S(2)}, u32[]{:S(2)}) collective-permute-start(bf16[2,32768]{1,0:T(2,128)(2,1)S(1)} %collective-permute-done.5), channel_id=1, source_target_pairs={{0,4},{4,8},{8,12},{12,16},{16,20},{20,24},{24,28},{28,0},{1,5},{5... | collective-permute-start | bytes 393224 | tf_op jit(solution)/shard_map/ppermute | solution.py:17
  79.2 1.8 copy-start.2
  171.4 3.0 %copy-start.4 = (f32[512,32]{0,1:T(8,128)S(1)}, f32[512,32]{0,1:T(8,128)}, u32[]{:S(2)}) copy-start(f32[512,32]{0,1:T(8,128)} %get-tuple-element.16) | copy-start | bytes 196612
  175.7 8.2 %copy-start.3 = (bf16[512,512]{0,1:T(8,128)(2,1)S(1)}, bf16[512,512]{0,1:T(8,128)(2,1)}, u32[]{:S(2)}) copy-start(bf16[512,512]{0,1:T(8,128)(2,1)} %fusion.12) | copy-start | bytes 1572868
Sparse Core Ops, SparseCore 0:
  9.5 59.3 all-gather.4
  71.0 50.3 all-gather.6
  123.6 47.7 all-gather.8
  173.3 49.5 all-gather.10
  227.2 29.5 reduce-scatter.1
